TPU v7x, 128 devices: a whole 4x4x4 slice. The times are simulated.
128 devices in a mesh: row: 8 (over z_hi, x), blk: 16 (over z_lo, y, core).
Axes of the slice: x: 4, y: 4, z: 4 (z_hi: 2, z_lo: 2; z = z_hi * 2 + z_lo), core: 2. Of those that a mesh axis runs over, the one named last changes fastest.
Arguments:
- spike_counts: int32 [16384, 2048], P(('row', 'blk')), may hold values from 0 to 23, as said below
- kernel_taps: int32 [16], replicated, may hold values from 1 to 8
- lag_bins: int32 [2], replicated, may hold values from 1 to 32, as said below
Outputs:
- correlogram: bfloat16 [2, 16384, 8, 2048], P(None, 'row', None, 'blk')
Inputs may be any that keep to these rules, and one draw needn't show every extreme that they name: `spike_counts`: neurons fire at different rates and share a common drive. `lag_bins`: the second lag equals 32; the first lies between 1 and 31.
All inputs are finite; a program needn't handle non-finite values.
Results may differ from a plain program's by a relative error of at most 0.0034.
Values may be sent and summed in bfloat16 or wider, within the bound.
A program may use at most 128 MiB of HBM per device.

v0:
```python
import jax
import jax.numpy as jnp
from jax import lax
from jax.sharding import PartitionSpec as P

NEURONS = 16384
BINS = 2048
TAPS = 16


def smoothed(spike_counts, kernel_taps):
    counts = spike_counts.astype(jnp.float32)
    weights = kernel_taps.astype(jnp.float32) / jnp.sum(kernel_taps.astype(jnp.float32))
    padded = jnp.pad(counts, ((0, 0), (TAPS - 1, 0)))
    result = jnp.zeros_like(counts)
    for delay in range(TAPS):
        result = result + weights[delay] * padded[:, TAPS - 1 - delay : TAPS - 1 - delay + BINS]
    return result


def later_bins(data, lag):
    padded = jnp.pad(data, ((0, 0), (0, BINS)))
    return lax.dynamic_slice_in_dim(padded, lag, BINS, 1)


def shards(spike_counts, kernel_taps, lag_bins):
    smooth = smoothed(spike_counts, kernel_taps)
    centred = smooth - jnp.mean(smooth, axis=1, keepdims=True)
    totals = lax.psum(jnp.sum(centred, axis=0), ("row", "blk"))
    residual_part = centred - (totals / NEURONS)[None, :]
    zscored = (
        residual_part
        * lax.rsqrt(jnp.mean(residual_part * residual_part, axis=1, keepdims=True) + 1e-05)
    ).astype(jnp.bfloat16)
    span_rows = zscored.shape[0]
    groups = lax.axis_size("row")
    columns = lax.all_gather(zscored, "row", axis=0, tiled=True)
    stacked = jnp.concatenate(
        [later_bins(columns, lag_bins[0]), later_bins(columns, lag_bins[1])], axis=0
    )
    piece = lax.all_gather(zscored, "blk", axis=0, tiled=True)
    product = jnp.dot(piece, stacked.T, preferred_element_type=jnp.float32) / BINS
    product = product.reshape(piece.shape[0], 2, groups, span_rows)
    return jnp.transpose(product, (1, 0, 2, 3)).astype(jnp.bfloat16)


def solution(mesh):
    placed = (P(("row", "blk"), None), P(), P())
    return jax.shard_map(
        shards, mesh=mesh, in_specs=placed, out_specs=P(None, "row", None, "blk"), check_vma=False
    )
```

profile of v0, /device:TPU:1, one launch (start us, length us, event | category | flops | bytes accessed | tf_op | source)
XLA Modules:
  0.0 258.9 jit_solution(15566849793997691235)
XLA Ops:
  6.5 0.0 copy-start
  6.5 0.0 all-gather.5.cloned.1.call-start
  6.5 1.3 convert_reduce_fusion
  7.8 1.3 convert_divide_fusion
  9.1 0.7 fusion.8
  9.8 1.3 convert_element_type.25
  11.2 14.1 %fusion.6 = (f32[128]{0:T(128)S(1)}, f32[128,2048]{1,0:T(8,128)S(1)}) fusion(f32[]{:T(128)} %bitcast.15, f32[]{:T(128)} %bitcast.14, f32[]{:T(128)} %bitcast.13, f32[]{:T(128)} %bitcast.12, f32[]{:T(128)} %bitcast.11, f32[]{:T(128)} %bitcast.10, f32[]{:T(128)} %bitcast.9, f32[]{:T(128)} %bitcast.8, f32[]{:T(128)} %bitcast.7, f32[]{:T(128)} %bitcast.6, ...), kind=kLoop, calls=%fused_computation.19 | loop fusion | flops 8388480 | bytes 2097728 | tf_op jit(solution)/shard_map/reduce_sum | solution.py:28
  25.3 0.2 subtract_reduce_fusion
  25.5 68.7 %psum.7 = f32[2048]{0:T(1024)S(1)} all-reduce(f32[2048]{0:T(1024)S(1)} %subtract_reduce_fusion), channel_id=1, replica_groups=mesh['row'=8,'blk'=16] {'row','blk'}, use_global_device_ids=true, to_apply=%region_3.4 | all-reduce | flops 2048 | bytes 16384 | tf_op jit(solution)/shard_map/psum | solution.py:29
  94.2 0.3 multiply_reduce_fusion
  94.5 1.0 multiply_convert_fusion.1
  95.5 0.0 all-gather.5.cloned.1.call-update
  95.6 0.2 all-gather.3.cloned.1.call-start
  95.8 0.5 all-gather.3.cloned.1.call-update
  96.3 0.0 copy-done
  96.3 0.6 fusion.7
  100.7 62.5 %all-gather.5.cloned.1.call-done = bf16[1024,2048]{1,0:T(8,128)(2,1)} async-done(((bf16[128,2048]{1,0:T(8,128)(2,1)}), bf16[1024,2048]{1,0:T(8,128)(2,1)}) %all-gather.5.cloned.1.call-update) | async-done | bytes 4194320 | tf_op jit(solution)/shard_map/all_gather | solution.py:37
  163.2 10.0 %pad_dynamic-slice_fusion.1 = (bf16[1024,2048]{1,0:T(8,128)(2,1)}, bf16[1024,2048]{1,0:T(8,128)(2,1)}) fusion(s32[]{:T(128)S(6)} %select_n.6, bf16[1024,2048]{1,0:T(8,128)(2,1)} %all-gather.5.cloned.1.call-done, s32[]{:T(128)S(6)} %select_n.7), kind=kLoop, calls=%fused_computation.2 | loop fusion | bytes 12582920 | tf_op jit(solution)/shard_map/dynamic_slice | solution.py:23
  173.2 42.5 %all-gather.3.cloned.1.call-done = bf16[2048,2048]{1,0:T(8,128)(2,1)} async-done(((bf16[128,2048]{1,0:T(8,128)(2,1)}), bf16[2048,2048]{1,0:T(8,128)(2,1)}) %all-gather.3.cloned.1.call-update) | async-done | bytes 8388624 | tf_op jit(solution)/shard_map/all_gather | solution.py:41
  215.7 23.8 %multiply_convert_fusion = bf16[2048,2048]{0,1:T(8,128)(2,1)} fusion(bf16[2048,2048]{1,0:T(8,128)(2,1)} %all-gather.3.cloned.1.call-done, bf16[1024,2048]{1,0:T(8,128)(2,1)} %get-tuple-element.8, bf16[1024,2048]{1,0:T(8,128)(2,1)} %get-tuple-element.7), kind=kOutput, calls=%fused_computation | convolution fusion | flops 17205035008 | bytes 25165824 | tf_op jit(solution)/shard_map/dot_general | solution.py:42
  239.5 12.6 %copy.4 = bf16[2048,2,8,128]{3,2,0,1:T(8,128)(2,1)} copy(bf16[2048,2,8,128]{0,3,2,1:T(8,128)(2,1)} %bitcast.21) | data formatting | bytes 16777216 | tf_op jit(solution)/shard_map/convert_element_type | solution.py:44
  (3 shorter events, 0.0 us)
Async XLA Ops:
  6.5 89.8 %copy-start = (s32[2]{0:T(128)S(1)}, s32[2]{0:T(128)}, u32[]{:S(2)}) copy-start(s32[2]{0:T(128)} %param.5) | copy-start | bytes 28
  6.5 156.7 %all-gather.5.cloned.1.call-start = ((), (), s32[]{:S(2)}) async-start(), calls=%async_computation.1 | async-start | bytes 4718592 | tf_op jit(solution)/shard_map/all_gather | solution.py:37
  95.6 120.2 %all-gather.3.cloned.1.call-start = ((), (), s32[]{:S(2)}) async-start(), calls=%async_computation | async-start | bytes 8912896 | tf_op jit(solution)/shard_map/all_gather | solution.py:41
Sparse Core Ops, SparseCore 0:
  95.7 67.5 all-gather.4
  165.0 50.7 all-gather.2
where the time goes:
time: 260 us; the launch traced here: 259 us
  waiting for transfers between devices  106 us (41%)
  blocking collectives  68.7 us (26%)
  local copies, waits for them, and re-layouts  23.9 us (9%)
  matrix products  23.8 us (9%)
  other arithmetic  19.5 us (8%)
  between operations  17.2 us (7%)
    psum x1, blocking collectives, shards(): totals = lax.psum(jnp.sum(centred, axis=0), ('row', 'blk'))  68.7 us
    all_gather x1, waiting for transfers between devices, shards(): columns = lax.all_gather(zscored, 'row', axis=0, tiled=True)  62.5 us
    all_gather x1, waiting for transfers between devices, shards(): piece = lax.all_gather(zscored, 'blk', axis=0, tiled=True)  42.5 us
    dot_general x1, matrix products, shards(): jnp.dot(piece, stacked.T, preferred_element_type=jnp.float32) / BINS  23.8 us
    reduce_sum x1, other arithmetic, shards(): centred = smooth - jnp.mean(smooth, axis=1, keepdims=True)  14.1 us
    convert_element_type x1, local copies, waits for them, and re-layouts, shards(): return jnp.transpose(product, (1, 0, 2, 3)).astype(jnp.bfloat16)  12.6 us
    dynamic_slice x1, local copies, waits for them, and re-layouts, later_bins(): return lax.dynamic_slice_in_dim(padded, lag, BINS, 1)  9.97 us
  transfers between devices with their start and end apart: 2, of which 2 were waited for; matrix products, arithmetic and copies ran while one was open for 4% of the time, Pallas kernels for 0%

commit v1 on v0

--- a/solution.py
+++ b/solution.py
@@ -2,6 +2,7 @@
 import jax.numpy as jnp
 from jax import lax
 from jax.sharding import PartitionSpec as P
+from jax.lax import psum
 
 NEURONS = 16384
 BINS = 2048
@@ -26,7 +27,7 @@
 def shards(spike_counts, kernel_taps, lag_bins):
     smooth = smoothed(spike_counts, kernel_taps)
     centred = smooth - jnp.mean(smooth, axis=1, keepdims=True)
-    totals = lax.psum(jnp.sum(centred, axis=0), ("row", "blk"))
+    totals = psum(psum(jnp.sum(centred, axis=0), axis_name="row"), axis_name="blk")
     residual_part = centred - (totals / NEURONS)[None, :]
     zscored = (
         residual_part

time: 260 us -> 242 us (0.931)
  blocking collectives: 68.7 us -> 53.7 us
  waiting for transfers between devices: 106 us -> 103 us
    psum x1 -> x2, blocking collectives: 68.7 us -> 53.7 us  [the longest x1 31.4 us: shards(): psum(psum(jnp.sum(centred, axis=0), axis_name='row'), axis_name='blk')]
where the time goes in v1:
time: 242 us
  waiting for transfers between devices  103 us (43%)
  blocking collectives  53.7 us (22%)
  local copies, waits for them, and re-layouts  23.9 us (10%)
  matrix products  23.8 us (10%)
  other arithmetic  19.5 us (8%)
  between operations  17.2 us (7%)
    all_gather x1, waiting for transfers between devices, shards(): columns = lax.all_gather(zscored, 'row', axis=0, tiled=True)  60.5 us
    all_gather x1, waiting for transfers between devices, shards(): piece = lax.all_gather(zscored, 'blk', axis=0, tiled=True)  42.5 us
    psum x1, blocking collectives, shards(): psum(psum(jnp.sum(centred, axis=0), axis_name='row'), axis_name='blk')  31.4 us
    dot_general x1, matrix products, shards(): jnp.dot(piece, stacked.T, preferred_element_type=jnp.float32) / BINS  23.8 us
    psum x1, blocking collectives, shards(): psum(jnp.sum(centred, axis=0), axis_name='row')  22.4 us
    reduce_sum x1, other arithmetic, shards(): centred = smooth - jnp.mean(smooth, axis=1, keepdims=True)  14.1 us
    convert_element_type x1, local copies, waits for them, and re-layouts, shards(): return jnp.transpose(product, (1, 0, 2, 3)).astype(jnp.bfloat16)  12.6 us
    dynamic_slice x1, local copies, waits for them, and re-layouts, later_bins(): return lax.dynamic_slice_in_dim(padded, lag, BINS, 1)  9.97 us
  transfers between devices with their start and end apart: 2, of which 2 were waited for; matrix products, arithmetic and copies ran while one was open for 4% of the time, Pallas kernels for 0%

profile of v1, /device:TPU:1, one launch (start us, length us, event | category | flops | bytes accessed | tf_op | source)
XLA Modules:
  0.0 241.8 jit_solution(10384331034966732726)
XLA Ops:
  6.5 0.0 copy-start
  6.5 0.0 all-gather.5.cloned.1.call-start
  6.5 1.3 convert_reduce_fusion
  7.8 1.3 convert_divide_fusion
  9.1 0.7 fusion.8
  9.8 1.3 convert_element_type.25
  11.2 14.1 %fusion.6 = (f32[128]{0:T(128)S(1)}, f32[128,2048]{1,0:T(8,128)S(1)}) fusion(f32[]{:T(128)} %bitcast.15, f32[]{:T(128)} %bitcast.14, f32[]{:T(128)} %bitcast.13, f32[]{:T(128)} %bitcast.12, f32[]{:T(128)} %bitcast.11, f32[]{:T(128)} %bitcast.10, f32[]{:T(128)} %bitcast.9, f32[]{:T(128)} %bitcast.8, f32[]{:T(128)} %bitcast.7, f32[]{:T(128)} %bitcast.6, ...), kind=kLoop, calls=%fused_computation.19 | loop fusion | flops 8388480 | bytes 2097728 | tf_op jit(solution)/shard_map/reduce_sum | solution.py:29
  25.3 0.2 subtract_reduce_fusion
  25.5 22.4 %psum.14 = f32[2048]{0:T(1024)S(1)} all-reduce(f32[2048]{0:T(1024)S(1)} %subtract_reduce_fusion), channel_id=1, replica_groups=mesh['row'=8,'blk'=16] {'row'}, use_global_device_ids=true, to_apply=%region_3.4 | all-reduce | flops 2048 | bytes 16384 | tf_op jit(solution)/shard_map/psum | solution.py:30
  47.8 31.4 %psum.15 = f32[2048]{0:T(1024)S(1)} all-reduce(f32[2048]{0:T(1024)S(1)} %psum.14), channel_id=1, replica_groups=mesh['row'=8,'blk'=16] {'blk'}, use_global_device_ids=true, to_apply=%region_4.5 | all-reduce | flops 2048 | bytes 16384 | tf_op jit(solution)/shard_map/psum | solution.py:30
  79.2 0.3 multiply_reduce_fusion
  79.5 1.0 multiply_convert_fusion.1
  80.6 0.0 all-gather.5.cloned.1.call-update
  80.6 0.2 all-gather.3.cloned.1.call-start
  80.8 0.5 all-gather.3.cloned.1.call-update
  81.3 0.0 copy-done
  81.4 0.6 fusion.7
  85.8 60.5 %all-gather.5.cloned.1.call-done = bf16[1024,2048]{1,0:T(8,128)(2,1)} async-done(((bf16[128,2048]{1,0:T(8,128)(2,1)}), bf16[1024,2048]{1,0:T(8,128)(2,1)}) %all-gather.5.cloned.1.call-update) | async-done | bytes 4194320 | tf_op jit(solution)/shard_map/all_gather | solution.py:38
  146.2 10.0 %pad_dynamic-slice_fusion.1 = (bf16[1024,2048]{1,0:T(8,128)(2,1)}, bf16[1024,2048]{1,0:T(8,128)(2,1)}) fusion(s32[]{:T(128)S(6)} %select_n.6, bf16[1024,2048]{1,0:T(8,128)(2,1)} %all-gather.5.cloned.1.call-done, s32[]{:T(128)S(6)} %select_n.7), kind=kLoop, calls=%fused_computation.2 | loop fusion | bytes 12582920 | tf_op jit(solution)/shard_map/dynamic_slice | solution.py:24
  156.2 42.5 %all-gather.3.cloned.1.call-done = bf16[2048,2048]{1,0:T(8,128)(2,1)} async-done(((bf16[128,2048]{1,0:T(8,128)(2,1)}), bf16[2048,2048]{1,0:T(8,128)(2,1)}) %all-gather.3.cloned.1.call-update) | async-done | bytes 8388624 | tf_op jit(solution)/shard_map/all_gather | solution.py:42
  198.7 23.8 %multiply_convert_fusion = bf16[2048,2048]{0,1:T(8,128)(2,1)} fusion(bf16[2048,2048]{1,0:T(8,128)(2,1)} %all-gather.3.cloned.1.call-done, bf16[1024,2048]{1,0:T(8,128)(2,1)} %get-tuple-element.8, bf16[1024,2048]{1,0:T(8,128)(2,1)} %get-tuple-element.7), kind=kOutput, calls=%fused_computation | convolution fusion | flops 17205035008 | bytes 25165824 | tf_op jit(solution)/shard_map/dot_general | solution.py:43
  222.4 12.6 %copy.4 = bf16[2048,2,8,128]{3,2,0,1:T(8,128)(2,1)} copy(bf16[2048,2,8,128]{0,3,2,1:T(8,128)(2,1)} %bitcast.21) | data formatting | bytes 16777216 | tf_op jit(solution)/shard_map/convert_element_type | solution.py:45
  (3 shorter events, 0.0 us)
Async XLA Ops:
  6.5 74.8 %copy-start = (s32[2]{0:T(128)S(1)}, s32[2]{0:T(128)}, u32[]{:S(2)}) copy-start(s32[2]{0:T(128)} %param.5) | copy-start | bytes 28
  6.5 139.7 %all-gather.5.cloned.1.call-start = ((), (), s32[]{:S(2)}) async-start(), calls=%async_computation.1 | async-start | bytes 4718592 | tf_op jit(solution)/shard_map/all_gather | solution.py:38
  80.6 118.1 %all-gather.3.cloned.1.call-start = ((), (), s32[]{:S(2)}) async-start(), calls=%async_computation | async-start | bytes 8912896 | tf_op jit(solution)/shard_map/all_gather | solution.py:42
Sparse Core Ops, SparseCore 0:
  80.7 65.4 all-gather.4
  147.9 50.7 all-gather.2
